TPU v7x, 32 devices: a whole 2x2x4 slice. The times are simulated.
32 devices in a mesh: vp: 4 (over y, x), cp: 2 (over core), ga: 4 (over z).
Axes of the slice: x: 2, y: 2, z: 4, core: 2. Of those that a mesh axis runs over, the one named last changes fastest.
Arguments:
- valence_wavefunction: bfloat16 [512, 24576], P(('vp', 'cp'), 'ga'), may hold values from -6 to 6
- cond_wave: bfloat16 [512, 24576], P(('vp', 'cp'), 'ga'), may hold values from -6 to 6
- screen_basis: bfloat16 [24576, 1024], P('ga'), may hold values from -0.0390625 to 0.0390625
- screen: float32 [1024], replicated, may hold values from 0.01 to 0.1
- coulomb: float32 [1024], replicated, may hold values from 0.02 to 0.2
- window_rows: int32 [2], replicated, may hold values from 0 to 1023
- tile_owner: int32 [48], P(('vp', 'cp')), may hold values from 0 to 4095, as said below
Outputs:
- kernel: float32 [2, 48, 4096], P(None, ('vp', 'cp'), 'ga')
Inputs may be any that keep to these rules, and one draw needn't show every extreme that they name: `tile_owner`: distinct pair-block indices; 0 and 4095 both occur.
All inputs are finite; a program needn't handle non-finite values.
Results may differ from a plain program's by a relative error of at most 0.02.
Values may be sent and summed in bfloat16 or wider, within the bound.
A program may use at most 64 MiB of HBM per device.

v0:
```python
import jax
import jax.numpy as jnp
from jax import lax
from jax.sharding import PartitionSpec as P

R = 1024
TV = 8
TC = 8
NCT = 64


def select_bands(wanted, shard_part):
    row_ids = jnp.arange(shard_part.shape[0], dtype=jnp.int32)
    chooser = (wanted[:, None] == row_ids[None, :]).astype(jnp.bfloat16)
    return jnp.dot(chooser, shard_part, preferred_element_type=jnp.float32)


def outer_rows(left_wavefunction, right_wave):
    product = (
        left_wavefunction.astype(jnp.float32)[..., :, None, :]
        * right_wave.astype(jnp.float32)[..., None, :, :]
    )
    return product.astype(jnp.bfloat16)


def contract(row_proj, col_proj, val_proj, cond_proj, screen_part, coulomb_part):
    exchange_term = jnp.einsum(
        "qacr,svdr->qsacvd", row_proj * coulomb_part, col_proj, precision=lax.Precision.HIGHEST
    )
    direct_term = jnp.einsum(
        "qsavr,qscdr->qsacvd", val_proj * screen_part, cond_proj, precision=lax.Precision.HIGHEST
    )
    total = 2.0 * exchange_term - direct_term
    return total.reshape(total.shape[0], total.shape[1], -1)


def shards(valence_wavefunction, cond_wave, screen_basis, screen, coulomb, window_rows, tile_owner):
    slot_count = tile_owner.shape[0]
    grid_count = valence_wavefunction.shape[1]
    pair_tiles = jnp.concatenate([window_rows, tile_owner])
    val_wanted = (
        (pair_tiles // NCT)[:, None] * TV + jnp.arange(TV, dtype=jnp.int32)[None, :]
    ).reshape(-1)
    conduction_wanted = (
        (pair_tiles % NCT)[:, None] * TC + jnp.arange(TC, dtype=jnp.int32)[None, :]
    ).reshape(-1)
    picked_val = select_bands(
        val_wanted, lax.all_gather(valence_wavefunction, ("vp", "cp"), axis=0, tiled=True)
    )
    picked_cond = select_bands(
        conduction_wanted, lax.all_gather(cond_wave, ("vp", "cp"), axis=0, tiled=True)
    )
    picked_val = picked_val.astype(jnp.bfloat16).reshape(2 + slot_count, TV, grid_count)
    picked_cond = picked_cond.astype(jnp.bfloat16).reshape(2 + slot_count, TC, grid_count)
    row_val = picked_val[:2]
    slot_valence = picked_val[2:]
    row_cond = picked_cond[:2]
    slot_cond = picked_cond[2:]
    row_rho = outer_rows(row_val, row_cond).reshape(2 * TV * TC, grid_count)
    col_rho = outer_rows(slot_valence, slot_cond).reshape(slot_count * TV * TC, grid_count)
    val_rho = outer_rows(row_val[:, None], slot_valence[None]).reshape(
        2 * slot_count * TV * TV, grid_count
    )
    cond_rho = outer_rows(row_cond[:, None], slot_cond[None]).reshape(
        2 * slot_count * TC * TC, grid_count
    )
    row_part = jnp.dot(row_rho, screen_basis, preferred_element_type=jnp.float32)
    col_part = jnp.dot(col_rho, screen_basis, preferred_element_type=jnp.float32)
    val_part = jnp.dot(val_rho, screen_basis, preferred_element_type=jnp.float32)
    cond_part = jnp.dot(cond_rho, screen_basis, preferred_element_type=jnp.float32)
    live_tile = (tile_owner[None, :] >= window_rows[:, None])[:, :, None]
    grid_groups = lax.axis_size("ga")
    rank_span = R // grid_groups
    rank_first = lax.axis_index("ga") * rank_span
    row_sum, col_sum, val_sum, cond_sum = (
        lax.psum_scatter(
            row_part.astype(jnp.bfloat16), "ga", scatter_dimension=1, tiled=True
        ).astype(jnp.float32),
        lax.psum_scatter(
            col_part.astype(jnp.bfloat16), "ga", scatter_dimension=1, tiled=True
        ).astype(jnp.float32),
        lax.psum_scatter(
            val_part.astype(jnp.bfloat16), "ga", scatter_dimension=1, tiled=True
        ).astype(jnp.float32),
        lax.psum_scatter(
            cond_part.astype(jnp.bfloat16), "ga", scatter_dimension=1, tiled=True
        ).astype(jnp.float32),
    )
    screen_part = lax.dynamic_slice_in_dim(screen, rank_first, rank_span, 0)
    coulomb_part = lax.dynamic_slice_in_dim(coulomb, rank_first, rank_span, 0)
    kernel = contract(
        row_sum.reshape(2, TV, TC, rank_span),
        col_sum.reshape(slot_count, TV, TC, rank_span),
        val_sum.reshape(2, slot_count, TV, TV, rank_span),
        cond_sum.reshape(2, slot_count, TC, TC, rank_span),
        screen_part,
        coulomb_part,
    )
    kernel = jnp.where(live_tile, kernel, jnp.zeros_like(kernel))
    return lax.psum_scatter(
        kernel.astype(jnp.bfloat16), "ga", scatter_dimension=2, tiled=True
    ).astype(jnp.float32)


def solution(mesh):
    in_specs = (
        P(("vp", "cp"), "ga"),
        P(("vp", "cp"), "ga"),
        P("ga", None),
        P(),
        P(),
        P(),
        P(("vp", "cp")),
    )
    out_specs = P(None, ("vp", "cp"), "ga")
    return jax.shard_map(shards, mesh=mesh, in_specs=in_specs, out_specs=out_specs, check_vma=False)
```

profile of v0, /device:TPU:0, one launch (start us, length us, event | category | flops | bytes accessed | tf_op | source)
XLA Modules:
  0.0 302.0 jit_solution(14764287237343330676)
XLA Ops:
  9.1 48.2 %all-gather.3.cloned.1.call-done = bf16[512,6144]{1,0:T(8,128)(2,1)} async-done(((bf16[64,6144]{1,0:T(8,128)(2,1)}), bf16[512,6144]{1,0:T(8,128)(2,1)}) %all-gather.3.cloned.1.call-update) | async-done | bytes 6291472 | tf_op jit(solution)/shard_map/all_gather | solution.py:48
  57.4 4.0 %convolution_convert_fusion.1 = bf16[64,6144]{1,0:T(8,128)(2,1)S(1)} fusion(bf16[512,6144]{1,0:T(8,128)(2,1)} %all-gather.3.cloned.1.call-done, s32[64]{0:T(128)S(1)} %add.72), kind=kOutput, calls=%fused_computation.4 | convolution fusion | flops 403079168 | bytes 7078144 | tf_op jit(solution)/shard_map/dot_general | solution.py:15
  61.5 43.1 %all-gather.5.cloned.1.call-done = bf16[512,6144]{1,0:T(8,128)(2,1)} async-done(((bf16[64,6144]{1,0:T(8,128)(2,1)}), bf16[512,6144]{1,0:T(8,128)(2,1)}) %all-gather.5.cloned.1.call-update) | async-done | bytes 6291472 | tf_op jit(solution)/shard_map/all_gather | solution.py:51
  104.7 4.0 %convolution_convert_fusion = bf16[64,6144]{1,0:T(8,128)(2,1)S(1)} fusion(bf16[512,6144]{1,0:T(8,128)(2,1)} %all-gather.5.cloned.1.call-done, s32[64]{0:T(128)S(1)} %add.77), kind=kOutput, calls=%fused_computation.3 | convolution fusion | flops 403079168 | bytes 7078144 | tf_op jit(solution)/shard_map/dot_general | solution.py:15
  109.1 7.1 %convolution_convert_fusion.5 = bf16[128,1024]{1,0:T(8,128)(2,1)} fusion(bf16[128,6144]{1,0:T(8,128)(2,1)S(1)} %bitcast.71, bf16[6144,1024]{1,0:T(8,128)(2,1)} %param.9), kind=kOutput, calls=%fused_computation.10 | convolution fusion | flops 1610743808 | bytes 14417920 | tf_op jit(solution)/shard_map/dot_general | solution.py:67
  116.2 5.7 %multiply_convert_fusion = bf16[2,6,8,8,6144]{4,3,2,1,0:T(8,128)(2,1)} fusion(f32[6,8,6144]{2,1,0:T(8,128)S(1)} %fusion.3, f32[2,8,6144]{2,1,0:T(8,128)S(1)} %fusion.6), kind=kLoop, calls=%fused_computation | loop fusion | flops 9437184 | bytes 11010048 | tf_op jit(solution)/shard_map/convert_element_type | solution.py:23
  121.9 15.7 %convolution_convert_fusion.2 = bf16[768,1024]{1,0:T(8,128)(2,1)} fusion(bf16[768,6144]{1,0:T(8,128)(2,1)} %bitcast.73, bf16[6144,1024]{1,0:T(8,128)(2,1)} %param.9), kind=kOutput, calls=%fused_computation.7 | convolution fusion | flops 9664462848 | bytes 23592960 | tf_op jit(solution)/shard_map/dot_general | solution.py:69
  137.6 5.7 %multiply_convert_fusion.1 = bf16[2,6,8,8,6144]{4,3,2,1,0:T(8,128)(2,1)} fusion(f32[6,8,6144]{2,1,0:T(8,128)S(1)} %fusion.2, f32[2,8,6144]{2,1,0:T(8,128)S(1)} %fusion.5), kind=kLoop, calls=%fused_computation.1 | loop fusion | flops 9437184 | bytes 11010048 | tf_op jit(solution)/shard_map/convert_element_type | solution.py:23
  143.5 15.7 %convolution_convert_fusion.3 = bf16[768,1024]{1,0:T(8,128)(2,1)} fusion(bf16[768,6144]{1,0:T(8,128)(2,1)} %bitcast.72, bf16[6144,1024]{1,0:T(8,128)(2,1)} %param.9), kind=kOutput, calls=%fused_computation.8 | convolution fusion | flops 9664462848 | bytes 23592960 | tf_op jit(solution)/shard_map/dot_general | solution.py:70
  160.2 9.1 %convolution_convert_fusion.4 = bf16[384,1024]{1,0:T(8,128)(2,1)} fusion(bf16[384,6144]{1,0:T(8,128)(2,1)S(1)} %bitcast.75, bf16[6144,1024]{1,0:T(8,128)(2,1)} %param.9), kind=kOutput, calls=%fused_computation.9 | convolution fusion | flops 4832231424 | bytes 18087936 | tf_op jit(solution)/shard_map/dot_general | solution.py:68
  171.2 0.9 convert_multiply_fusion.2
  172.0 6.9 %reduce-scatter.14.cloned.1.call-done = bf16[768,256]{1,0:T(8,128)(2,1)} async-done(((bf16[768,1024]{1,0:T(8,128)(2,1)}), bf16[768,256]{1,0:T(8,128)(2,1)}) %reduce-scatter.14.cloned.1.call-update) | async-done | bytes 393232 | tf_op jit(solution)/shard_map/reduce_scatter | solution.py:82
  178.9 36.5 %reduce-scatter.12.cloned.1.call-done = bf16[768,256]{1,0:T(8,128)(2,1)} async-done(((bf16[768,1024]{1,0:T(8,128)(2,1)}), bf16[768,256]{1,0:T(8,128)(2,1)}) %reduce-scatter.12.cloned.1.call-update) | async-done | bytes 393232 | tf_op jit(solution)/shard_map/reduce_scatter | solution.py:85
  215.4 6.3 %fusion = f32[2,6,8,8,8,8]{5,3,4,2,1,0:T(8,128)} fusion(bf16[2,6,8,8,256,1]{4,3,5,2,1,0:T(8,128)(2,1)} %bitcast.78, bf16[2,6,8,8,256]{4,3,2,1,0:T(8,128)(2,1)} %bitcast.77, f32[256]{0:T(256)S(1)} %dynamic_slice.7), kind=kOutput, calls=%fused_computation.11 | convolution fusion | flops 151388160 | bytes 984064 | tf_op jit(solution)/shard_map/qsavr,qscdr->qsacvd/dot_general | solution.py:30
  221.6 4.3 %copy.11 = f32[2,6,8,8,8,8]{2,3,4,0,5,1:T(8,128)S(1)} copy(f32[2,6,8,8,8,8]{5,3,4,2,1,0:T(8,128)} %fusion) | data formatting | bytes 393216 | tf_op jit(solution)/shard_map/qsavr,qscdr->qsacvd/dot_general | solution.py:30
  226.0 13.6 %reduce-scatter.8.cloned.1.call-done = bf16[384,256]{1,0:T(8,128)(2,1)} async-done(((bf16[384,1024]{1,0:T(8,128)(2,1)}), bf16[384,256]{1,0:T(8,128)(2,1)}) %reduce-scatter.8.cloned.1.call-update) | async-done | bytes 196624 | tf_op jit(solution)/shard_map/reduce_scatter | solution.py:79
  239.6 3.5 %bitcast_subtract_fusion = bf16[2,6,8,8,8,8]{3,5,2,0,4,1:T(8,128)(2,1)} fusion(f32[2,6,8,8,8,8]{2,3,4,0,5,1:T(8,128)S(1)} %copy.11, bf16[6,8,8,256,1,1]{3,2,5,4,1,0:T(8,128)(2,1)} %bitcast.79, f32[2,8,8,256,1,1]{3,2,1,0,5,4:T(8,128)S(1)} %bitcast.76), kind=kOutput, calls=%fused_computation.5 | convolution fusion | flops 151142400 | bytes 622592 | tf_op jit(solution)/shard_map/qacr,svdr->qsacvd/dot_general | solution.py:27
  243.0 2.1 copy.12
  245.2 1.7 reshape.286
  247.0 7.4 %copy.17 = bf16[2,6,4096]{0,1,2:T(8,128)(2,1)} copy(bf16[2,6,4096]{2,0,1:T(2,128)(2,1)S(1)} %select_convert_fusion) | data formatting | bytes 196608
  254.4 9.5 %reshape.297 = bf16[4096,12]{1,0:T(8,128)(2,1)} reshape(bf16[4096,6,2]{2,1,0:T(8,128)(2,1)} %bitcast.70) | data formatting | bytes 196608
  263.9 27.0 %reduce-scatter.16.cloned.1.call-done = bf16[1024,12]{1,0:T(8,128)(2,1)} async-done(((bf16[4096,12]{1,0:T(8,128)(2,1)}), bf16[1024,12]{1,0:T(8,128)(2,1)}) %reduce-scatter.16.cloned.1.call-update) | async-done | bytes 24592
  290.9 2.4 reshape.298
  293.3 1.2 copy.18
  (36 shorter events, 6.9 us)
Async XLA Ops:
  6.5 50.8 %all-gather.3.cloned.1.call-start = ((), (), s32[]{:S(2)}) async-start(), calls=%async_computation.5 | async-start | bytes 7077888 | tf_op jit(solution)/shard_map/all_gather | solution.py:48
  7.3 97.4 %all-gather.5.cloned.1.call-start = ((), (), s32[]{:S(2)}) async-start(), calls=%async_computation.6 | async-start | bytes 7077888 | tf_op jit(solution)/shard_map/all_gather | solution.py:51
  8.0 163.2 %reduce-scatter.10.cloned.1.call-start = ((), (), s32[]{:S(2)}) async-start(), calls=%async_computation.8 | async-start | bytes 327680 | tf_op jit(solution)/shard_map/reduce_scatter | solution.py:76
  116.2 62.7 %reduce-scatter.14.cloned.1.call-start = ((), (), s32[]{:S(2)}) async-start(), calls=%async_computation.10 | async-start | bytes 1966080 | tf_op jit(solution)/shard_map/reduce_scatter | solution.py:82
  143.3 72.1 %reduce-scatter.12.cloned.1.call-start = ((), (), s32[]{:S(2)}) async-start(), calls=%async_computation.9 | async-start | bytes 1966080 | tf_op jit(solution)/shard_map/reduce_scatter | solution.py:85
  159.2 80.3 %reduce-scatter.8.cloned.1.call-start = ((), (), s32[]{:S(2)}) async-start(), calls=%async_computation.7 | async-start | bytes 983040 | tf_op jit(solution)/shard_map/reduce_scatter | solution.py:79
  160.1 10.9 %copy-start = (s32[6]{0:T(128)S(1)}, s32[6]{0:T(128)}, u32[]{:S(2)}) copy-start(s32[6]{0:T(128)} %param.13) | copy-start | bytes 76
  160.2 10.9 %copy-start.1 = (s32[2]{0:T(128)S(1)}, s32[2]{0:T(128)}, u32[]{:S(2)}) copy-start(s32[2]{0:T(128)} %param.12) | copy-start | bytes 28
  169.3 121.6 %reduce-scatter.16.cloned.1.call-start = ((), (), s32[]{:S(2)}) async-start(), calls=%async_computation.11 | async-start | bytes 1310720
Sparse Core Ops, SparseCore 0:
  9.2 48.1 all-gather.2
  59.2 45.3 all-gather.4
  116.3 19.9 reduce-scatter.9
  143.4 35.4 reduce-scatter.13
  181.0 34.2 reduce-scatter.11
  217.5 21.9 reduce-scatter.7
  264.0 26.8 reduce-scatter.15
where the time goes:
time: 303 us; the launch traced here: 302 us
  waiting for transfers between devices  177 us (58%)
  matrix products  65.4 us (22%)
  local copies, waits for them, and re-layouts  30.3 us (10%)
  other arithmetic  15.2 us (5%)
  between operations  13.6 us (4%)
    all_gather x1, waiting for transfers between devices, shards(): lax.all_gather(valence_wavefunction, ('vp', 'cp'), axis=0, tiled=True)  48.2 us
    all_gather x1, waiting for transfers between devices, shards(): lax.all_gather(cond_wave, ('vp', 'cp'), axis=0, tiled=True)  43.1 us
    reduce_scatter x1, waiting for transfers between devices, shards(): lax.psum_scatter(cond_part.astype(jnp.bfloat16), 'ga', scatter_dimension=...  36.5 us
    unnamed x8, waiting for transfers between devices  28.5 us
    unnamed x8, local copies, waits for them, and re-layouts  20.5 us
    dot_general x1, matrix products, shards(): jnp.dot(cond_rho, screen_basis, preferred_element_type=jnp.float32)  15.7 us
    dot_general x1, matrix products, shards(): jnp.dot(val_rho, screen_basis, preferred_element_type=jnp.float32)  15.7 us
    reduce_scatter x1, waiting for transfers between devices, shards(): lax.psum_scatter(col_part.astype(jnp.bfloat16), 'ga', scatter_dimension=1...  13.6 us
  transfers between devices with their start and end apart: 7, of which 6 were waited for; matrix products, arithmetic and copies ran while one was open for 23% of the time, Pallas kernels for 0%

commit v1 on v0

v1 whole, which is shorter than its diff:
```python
import functools
import jax
import jax.numpy as jnp
from jax import lax
from jax.experimental import pallas as pl
from jax.experimental.pallas import tpu as pltpu
from jax.sharding import PartitionSpec as P

TV = 8
TC = 8
NCT = 64
LAG = 2
ROW_TILES = 2


def select_bands(wanted, shard_part):
    row_ids = jnp.arange(shard_part.shape[0], dtype=jnp.int32)
    chooser = (wanted[:, None] == row_ids[None, :]).astype(jnp.bfloat16)
    return jnp.dot(chooser, shard_part, preferred_element_type=jnp.float32)


def pair_rows(rho, first, left, right, lanes):
    for i in range(len(left)):
        rho[pl.ds(first + 16 * i, 16), lanes] = left[i] * right


def spread(tile):
    out = []
    for i in range(0, tile.shape[0], 2):
        two = [jnp.broadcast_to(tile[i + j : i + j + 1], (8, tile.shape[1])) for j in range(2)]
        out.append(jnp.concatenate(two, axis=0).astype(jnp.bfloat16))
    return out


def twice(tile):
    return jnp.concatenate([tile, tile], axis=0).astype(jnp.bfloat16)


def dot_t(a, b):
    return lax.dot_general(a, b, (((1,), (1,)), ((), ())), preferred_element_type=jnp.float32)


def weighted_dot(a, weight, b):
    scaled = a.astype(jnp.float32) * weight
    high = scaled.astype(jnp.bfloat16)
    low = (scaled - high.astype(jnp.float32)).astype(jnp.bfloat16)
    return dot_t(high, b) + dot_t(low, b)


def tiles_kernel(
    n, slots, val_ref, cond_ref, basis_hbm, screen_ref, coulomb_ref, exch_ref, direct_ref,
    basis, rho, acc, own, got, ex_own, dr_own, ex_send, dr_send, ex_got, dr_got,
    basis_sem, send_sem, recv_sem, fin_send, fin_recv,
):
    z = lax.axis_index("ga")
    grid, rank = basis_hbm.shape
    steps, rows, width = own.shape[1:]
    halves = rank // (2 * width)
    ends = (0, n - 1)
    block = TV * TC

    copies = []
    for c in range(2 * halves):
        cols = pl.ds(c * width, width)
        copy = pltpu.make_async_copy(basis_hbm.at[:, cols], basis.at[:, cols], basis_sem.at[c])
        copy.start()
        copies.append(copy)

    barrier = pltpu.get_barrier_semaphore()
    for other in range(1, n):
        pl.semaphore_signal(
            barrier, inc=1, device_id={"ga": lax.rem(z + other, n)}, device_id_type=pl.DeviceIdType.MESH
        )

    lane = 256

    def densities(g, _):
        lanes = pl.ds(pl.multiple_of(g * lane, lane), lane)
        val = val_ref[:, lanes].astype(jnp.float32)
        cond = cond_ref[:, lanes].astype(jnp.float32)
        row_val = [spread(val[q * TV : (q + 1) * TV]) for q in range(ROW_TILES)]
        row_cond = [spread(cond[q * TC : (q + 1) * TC]) for q in range(ROW_TILES)]
        for q in range(ROW_TILES):
            pair_rows(rho, q * block, row_val[q], twice(cond[q * TC : (q + 1) * TC]), lanes)
        for s in range(slots):
            at = (ROW_TILES + s) * 8
            slot_val, slot_cond = val[at : at + TV], cond[at : at + TC]
            right_val, right_cond = twice(slot_val), twice(slot_cond)
            pair_rows(rho, (ROW_TILES + s) * block, spread(slot_val), right_cond, lanes)
            first = (ROW_TILES + slots + 2 * ROW_TILES * s) * block
            for q in range(ROW_TILES):
                pair_rows(rho, first + q * block, row_val[q], right_val, lanes)
                pair_rows(rho, first + (ROW_TILES + q) * block, row_cond[q], right_cond, lanes)
        return 0

    lax.fori_loop(0, grid // lane, densities, 0)
    pl.semaphore_wait(barrier, n - 1)

    depth = 1024
    toward = (-1, 1)

    def hop(way, k):
        return pltpu.make_async_remote_copy(
            src_ref=own.at[way, k],
            dst_ref=got.at[way, k],
            send_sem=send_sem.at[way, k],
            recv_sem=recv_sem.at[way, k],
            device_id={"ga": lax.rem(z + toward[way] + n, n)},
            device_id_type=pl.DeviceIdType.MESH,
        )

    far = (n - 1 - z, z)

    def step(i, _):
        @pl.when(i < steps)
        def _():
            first = pl.multiple_of((i // halves) * rows, rows)
            for way in range(2):
                part = way * halves + lax.rem(i, halves)
                column = pl.multiple_of(part * width, width)

                for c in range(halves):
                    @pl.when(i == c)
                    def _():
                        copies[way * halves + c].wait()

                acc[...] = jnp.zeros_like(acc)

                def deep(k, _):
                    at = pl.multiple_of(k * depth, depth)
                    acc[...] += jnp.dot(
                        rho[pl.ds(first, rows), pl.ds(at, depth)],
                        basis[pl.ds(at, depth), pl.ds(column, width)],
                        preferred_element_type=jnp.float32,
                    )
                    return 0

                lax.fori_loop(0, grid // depth, deep, 0)
                own[way, i] = acc[...].astype(jnp.bfloat16)

        for way in range(2):
            k = i - LAG * far[way]

            @pl.when(jnp.logical_and(k >= 0, k < steps))
            def _():
                @pl.when(far[way] > 0)
                def _():
                    hop(way, k).wait_recv()
                    total = own[way, k].astype(jnp.float32) + got[way, k].astype(jnp.float32)
                    own[way, k] = total.astype(jnp.bfloat16)

                @pl.when(z != ends[way])
                def _():
                    hop(way, k).start()

        return 0

    lax.fori_loop(0, steps + LAG * (n - 1), step, 0)

    share = block // n

    def give(way, k):
        return [
            pltpu.make_async_remote_copy(
                src_ref=sent.at[k],
                dst_ref=there.at[way],
                send_sem=fin_send.at[k, j],
                recv_sem=fin_recv.at[way, j],
                device_id={"ga": k},
                device_id_type=pl.DeviceIdType.MESH,
            )
            for j, (sent, there) in enumerate(((ex_send, ex_got), (dr_send, dr_got)))
        ]

    for way in range(2):
        @pl.when(z == ends[way])
        def _():
            exchange = jnp.zeros(ex_own.shape, jnp.float32)
            for c in range(halves):
                weight = coulomb_ref[:, pl.ds((way * halves + c) * width, width)]
                left = own[way, c, pl.ds(0, ROW_TILES * block), :]
                right = own[way, c, pl.ds(ROW_TILES * block, slots * block), :]
                exchange += weighted_dot(left, weight, right)
            ex_own[...] = exchange
            wide = ROW_TILES * block
            for s in range(slots):
                first = (ROW_TILES + slots + 2 * ROW_TILES * s) * block
                job, at = first // rows, first % rows
                direct = jnp.zeros((wide, wide), jnp.float32)
                for c in range(halves):
                    weight = screen_ref[:, pl.ds((way * halves + c) * width, width)]
                    left = own[way, job * halves + c, pl.ds(at, wide), :]
                    right = own[way, job * halves + c, pl.ds(at + wide, wide), :]
                    direct += weighted_dot(left, weight, right)
                column = lax.broadcasted_iota(jnp.int32, (block, wide), 1)
                dr_own[s] = jnp.where(column < block, direct[:block], direct[block:])
            for k in range(n):
                if k != ends[way]:
                    for q in range(ROW_TILES):
                        ex_send[k, q] = ex_own[pl.ds(q * block + k * share, share), :].astype(jnp.bfloat16)
                    dr_send[k] = dr_own[:, pl.ds(k * share, share), :].astype(jnp.bfloat16)
                    for copy in give(way, k):
                        copy.start()
            for q in range(ROW_TILES):
                exch_ref[q] = ex_own[pl.ds(q * block + ends[way] * share, share), :]
            direct_ref[...] = dr_own[:, pl.ds(ends[way] * share, share), :]

    for way in range(2):
        @pl.when(z != ends[way])
        def _():
            for copy in give(way, 0):
                copy.wait_recv()
            here = ends[1 - way]

            def put(fresh):
                ex_part = ex_got[way].astype(jnp.float32)
                dr_part = dr_got[way].astype(jnp.float32)
                exch_ref[...] = ex_part if fresh else exch_ref[...] + ex_part
                direct_ref[...] = dr_part if fresh else direct_ref[...] + dr_part

            if way == 0:
                pl.when(z == here)(lambda: put(False))
                pl.when(z != here)(lambda: put(True))
            else:
                put(False)

    for way in range(2):
        @pl.when(z != ends[way])
        def _():
            def drain(k, _):
                hop(way, k).wait_send()
                return 0

            lax.fori_loop(0, steps, drain, 0)

        @pl.when(z == ends[way])
        def _():
            for k in range(n):
                if k != ends[way]:
                    for copy in give(way, k):
                        copy.wait_send()


def make_tiles(n, slots, val, cond, basis, screen, coulomb):
    grid, rank = basis.shape
    width = rank // 4
    block = TV * TC
    rows = (ROW_TILES + slots) * block
    total = (ROW_TILES + slots + 2 * ROW_TILES * slots) * block
    steps = (total // rows) * 2
    share = block // n
    vmem = pl.BlockSpec(memory_space=pltpu.VMEM)
    bf16, f32 = jnp.bfloat16, jnp.float32
    return pl.pallas_call(
        functools.partial(tiles_kernel, n, slots),
        out_shape=(
            jax.ShapeDtypeStruct((ROW_TILES, share, slots * block), f32),
            jax.ShapeDtypeStruct((slots, share, ROW_TILES * block), f32),
        ),
        in_specs=[vmem, vmem, pl.BlockSpec(memory_space=pl.ANY), vmem, vmem],
        out_specs=(vmem, vmem),
        scratch_shapes=[
            pltpu.VMEM((grid, rank), bf16),
            pltpu.VMEM((total, grid), bf16),
            pltpu.VMEM((rows, width), f32),
            pltpu.VMEM((2, steps, rows, width), bf16),
            pltpu.VMEM((2, steps, rows, width), bf16),
            pltpu.VMEM((ROW_TILES * block, slots * block), f32),
            pltpu.VMEM((slots, block, ROW_TILES * block), f32),
            pltpu.VMEM((n, ROW_TILES, share, slots * block), bf16),
            pltpu.VMEM((n, slots, share, ROW_TILES * block), bf16),
            pltpu.VMEM((2, ROW_TILES, share, slots * block), bf16),
            pltpu.VMEM((2, slots, share, ROW_TILES * block), bf16),
            pltpu.SemaphoreType.DMA((4,)),
            pltpu.SemaphoreType.DMA((2, steps)),
            pltpu.SemaphoreType.DMA((2, steps)),
            pltpu.SemaphoreType.DMA((n, 2)),
            pltpu.SemaphoreType.DMA((2, 2)),
        ],
        compiler_params=pltpu.CompilerParams(
            collective_id=0, has_side_effects=True, vmem_limit_bytes=67043328
        ),
    )(val, cond, basis, screen, coulomb)


def shards(valence_wavefunction, cond_wave, screen_basis, screen, coulomb, window_rows, tile_owner):
    slots = tile_owner.shape[0]
    n = lax.axis_size("ga")
    pair_tiles = jnp.concatenate([window_rows, tile_owner])
    val_wanted = (
        (pair_tiles // NCT)[:, None] * TV + jnp.arange(TV, dtype=jnp.int32)[None, :]
    ).reshape(-1)
    cond_wanted = (
        (pair_tiles % NCT)[:, None] * TC + jnp.arange(TC, dtype=jnp.int32)[None, :]
    ).reshape(-1)
    val = select_bands(
        val_wanted, lax.all_gather(valence_wavefunction, ("vp", "cp"), axis=0, tiled=True)
    ).astype(jnp.bfloat16)
    cond = select_bands(
        cond_wanted, lax.all_gather(cond_wave, ("vp", "cp"), axis=0, tiled=True)
    ).astype(jnp.bfloat16)
    exchange, direct = make_tiles(n, slots, val, cond, screen_basis, screen[None], coulomb[None])
    v = TV // n
    exchange = exchange.reshape(2, v, TC, slots, TV, TC).transpose(0, 3, 1, 2, 4, 5)
    direct = direct.reshape(slots, v, TV, 2, TC, TC).transpose(3, 0, 1, 4, 2, 5)
    kernel = (2.0 * exchange - direct).reshape(2, slots, -1)
    live = (tile_owner[None, :] >= window_rows[:, None])[:, :, None]
    return jnp.where(live, kernel, jnp.zeros_like(kernel))


def solution(mesh):
    in_specs = (
        P(("vp", "cp"), "ga"),
        P(("vp", "cp"), "ga"),
        P("ga", None),
        P(),
        P(),
        P(),
        P(("vp", "cp")),
    )
    out_specs = P(None, ("vp", "cp"), "ga")
    return jax.shard_map(shards, mesh=mesh, in_specs=in_specs, out_specs=out_specs, check_vma=False)
```

time: 303 us -> 209 us (0.69)
  Pallas kernels: 0 us -> 87.9 us
  waiting for transfers between devices: 177 us -> 90 us
  matrix products: 65.4 us -> 9.92 us
  local copies, waits for them, and re-layouts: 30.3 us -> 2.49 us
  other arithmetic: 15.2 us -> 4.75 us
    pallas_call x0 -> x1, Pallas kernels: none -> 87.9 us  [make_tiles(): pl.pallas_call(functools.partial(tiles_kernel, n, slots), out_shape=(jax....]
    dot_general x6 -> x0, matrix products: 57.3 us -> none  [the longest x1 15.7 us: shards(): jnp.dot(cond_rho, screen_basis, preferred_element_type=jnp.float32)]
    reduce_scatter x4 -> x0, waiting for transfers between devices: 56.9 us -> none  [the longest x1 36.5 us: shards(): lax.psum_scatter(cond_part.astype(jnp.bfloat16), 'ga', scatter_dimension=...]
    unnamed x8 -> x2, waiting for transfers between devices: 28.5 us -> 1.41 us
    unnamed x8 -> x2, local copies, waits for them, and re-layouts: 20.5 us -> 0.01 us
    convert_element_type x10 -> x0, other arithmetic: 13.4 us -> none  [the longest x4 12.4 us: outer_rows(): return product.astype(jnp.bfloat16)]
    dot_general x1 -> x0, local copies, waits for them, and re-layouts: 4.34 us -> none  [contract(): jnp.einsum('qsavr,qscdr->qsacvd', val_proj * screen_part, cond_proj, prec...]
  transfers between devices with their start and end apart: 7 -> 2, of which waited for: 6 -> 2; matrix products, arithmetic and copies ran while one was open for 23% -> 4% of each run, Pallas kernels for 0% -> 0%
where the time goes in v1:
time: 209 us
  waiting for transfers between devices  90 us (43%)
  Pallas kernels  87.9 us (42%)
  between operations  13.5 us (6%)
  matrix products  9.92 us (5%)
  other arithmetic  4.75 us (2%)
  local copies, waits for them, and re-layouts  2.49 us (1%)
    pallas_call x1, Pallas kernels, make_tiles(): pl.pallas_call(functools.partial(tiles_kernel, n, slots), out_shape=(jax....  87.9 us
    all_gather x1, waiting for transfers between devices, shards(): lax.all_gather(valence_wavefunction, ('vp', 'cp'), axis=0, tiled=True)  46.3 us
    all_gather x1, waiting for transfers between devices, shards(): lax.all_gather(cond_wave, ('vp', 'cp'), axis=0, tiled=True)  42.3 us
    dot_general x2, matrix products, select_bands(): return jnp.dot(chooser, shard_part, preferred_element_type=jnp.float32)  9.92 us
  transfers between devices with their start and end apart: 2, of which 2 were waited for; matrix products, arithmetic and copies ran while one was open for 4% of the time, Pallas kernels for 0%

profile of v1, /device:TPU:0, one launch (start us, length us, event | category | flops | bytes accessed | tf_op | source)
XLA Modules:
  0.0 208.6 jit_solution(76560033543841465)
XLA Ops:
  6.5 0.0 all-gather.3.cloned.1.call-start
  6.5 0.7 all-gather.3.cloned.1.call-update
  7.3 0.0 all-gather.5.cloned.1.call-start
  7.3 0.7 all-gather.5.cloned.1.call-update
  8.0 0.8 fusion.2
  8.8 0.8 fusion.3
  9.5 0.1 iota_add_fusion.1
  9.6 0.1 add.58
  9.7 0.1 iota_add_fusion
  9.7 0.1 add.63
  9.8 1.3 broadcast_compare_fusion
  11.1 46.3 %all-gather.3.cloned.1.call-done = bf16[512,6144]{1,0:T(8,128)(2,1)} async-done(((bf16[64,6144]{1,0:T(8,128)(2,1)}), bf16[512,6144]{1,0:T(8,128)(2,1)}) %all-gather.3.cloned.1.call-update) | async-done | bytes 6291472 | tf_op jit(solution)/shard_map/all_gather | solution.py:297
  57.4 5.0 %convolution_convert_fusion.1.val_ref = bf16[64,6144]{1,0:T(8,128)(2,1)} fusion(bf16[512,6144]{1,0:T(8,128)(2,1)} %all-gather.3.cloned.1.call-done, s32[64]{0:T(128)S(1)} %add.58), kind=kOutput, calls=%fused_computation.1 | convolution fusion | flops 403079168 | bytes 7078144 | tf_op jit(solution)/shard_map/dot_general | solution.py:19
  62.4 42.3 %all-gather.5.cloned.1.call-done = bf16[512,6144]{1,0:T(8,128)(2,1)} async-done(((bf16[64,6144]{1,0:T(8,128)(2,1)}), bf16[512,6144]{1,0:T(8,128)(2,1)}) %all-gather.5.cloned.1.call-update) | async-done | bytes 6291472 | tf_op jit(solution)/shard_map/all_gather | solution.py:300
  104.7 4.9 %convolution_convert_fusion.cond_ref = bf16[64,6144]{1,0:T(8,128)(2,1)} fusion(bf16[512,6144]{1,0:T(8,128)(2,1)} %all-gather.5.cloned.1.call-done, s32[64]{0:T(128)S(1)} %add.63), kind=kOutput, calls=%fused_computation | convolution fusion | flops 403079168 | bytes 7078144 | tf_op jit(solution)/shard_map/dot_general | solution.py:19
  109.7 87.9 %shard_map.73 = (f32[2,16,384]{2,1,0:T(8,128)}, f32[6,16,128]{2,1,0:T(8,128)}) custom-call(bf16[64,6144]{1,0:T(8,128)(2,1)} %convolution_convert_fusion.1.val_ref, bf16[64,6144]{1,0:T(8,128)(2,1)} %convolution_convert_fusion.cond_ref, bf16[6144,1024]{1,0:T(8,128)(2,1)} %basis_hbm.1, f32[1,1024]{1,0:T(1,128)} %bitcast.12, f32[1,1024]{1,0:T(1,128)} %bitcast.13), custom_call_target="tpu_custom_call" | custom-call | tf_op jit(solution)/shard_map/pallas_call | solution.py:254
  197.6 0.0 copy-start
  197.6 0.8 broadcast_multiply_fusion
  198.4 0.4 mul.32
  198.9 1.2 reshape.182
  200.1 0.3 bitcast_subtract_fusion
  200.4 0.2 copy.9
  200.7 0.4 reshape.183
  201.1 0.7 broadcast_select_fusion
  (1 shorter events, 0.0 us)
Async XLA Ops:
  6.5 50.9 %all-gather.3.cloned.1.call-start = ((), (), s32[]{:S(2)}) async-start(), calls=%async_computation | async-start | bytes 7077888 | tf_op jit(solution)/shard_map/all_gather | solution.py:297
  7.3 97.5 %all-gather.5.cloned.1.call-start = ((), (), s32[]{:S(2)}) async-start(), calls=%async_computation.1 | async-start | bytes 7077888 | tf_op jit(solution)/shard_map/all_gather | solution.py:300
  197.6 3.4 %copy-start = (pred[2,6]{0,1:T(8,128)(4,1)S(1)}, pred[2,6]{0,1:T(8,128)(4,1)}, u32[]{:S(2)}) copy-start(pred[2,6]{0,1:T(8,128)(4,1)} %broadcast_compare_fusion) | copy-start | bytes 40
Sparse Core Ops, SparseCore 0:
  9.2 48.1 all-gather.2
  59.3 45.3 all-gather.4

commit v2 on v1

--- a/solution.py
+++ b/solution.py
@@ -13,12 +13,6 @@
 ROW_TILES = 2
 
 
-def select_bands(wanted, shard_part):
-    row_ids = jnp.arange(shard_part.shape[0], dtype=jnp.int32)
-    chooser = (wanted[:, None] == row_ids[None, :]).astype(jnp.bfloat16)
-    return jnp.dot(chooser, shard_part, preferred_element_type=jnp.float32)
-
-
 def pair_rows(rho, first, left, right, lanes):
     for i in range(len(left)):
         rho[pl.ds(first + 16 * i, 16), lanes] = left[i] * right
@@ -48,8 +42,9 @@
 
 
 def tiles_kernel(
-    n, slots, val_ref, cond_ref, basis_hbm, screen_ref, coulomb_ref, exch_ref, direct_ref,
-    basis, rho, acc, own, got, ex_own, dr_own, ex_send, dr_send, ex_got, dr_got,
+    n, n_vp, n_cp, slots, val_hbm, cond_hbm, wanted_ref, basis_hbm, screen_ref, coulomb_ref,
+    exch_ref, direct_ref, wanted, near, picked, sent, came, total, ready, basis, rho, acc, own, got, ex_own, dr_own, ex_send, dr_send, ex_got, dr_got,
+    want_send, want_recv, near_send, near_recv, cross_send, cross_recv, give_send, give_recv,
     basis_sem, send_sem, recv_sem, fin_send, fin_recv,
 ):
     z = lax.axis_index("ga")
@@ -72,12 +67,146 @@
             barrier, inc=1, device_id={"ga": lax.rem(z + other, n)}, device_id_type=pl.DeviceIdType.MESH
         )
 
-    lane = 256
-
-    def densities(g, _):
-        lanes = pl.ds(pl.multiple_of(g * lane, lane), lane)
-        val = val_ref[:, lanes].astype(jnp.float32)
-        cond = cond_ref[:, lanes].astype(jnp.float32)
+    vp, cp = lax.axis_index("vp"), lax.axis_index("cp")
+    group = n_vp * n_cp
+    me = vp * n_cp + cp
+    for other in range(1, group):
+        peer = lax.rem(me + other, group)
+        pl.semaphore_signal(
+            barrier, inc=1, device_id={"vp": peer // n_cp, "cp": lax.rem(peer, n_cp)},
+            device_id_type=pl.DeviceIdType.MESH,
+        )
+    pl.semaphore_wait(barrier, n - 1 + group - 1)
+
+    waves = (val_hbm, cond_hbm)
+    bands = val_hbm.shape[0]
+    chip = n_cp * bands
+    part = grid // n_cp
+    pieces = near_send.shape[-1]
+    piece = part // pieces
+    side = lax.rem(cp, 2)
+    flips = (vp + 1 - 2 * lax.rem(vp, 2), lax.rem(vp + n_vp // 2, n_vp))
+    peer_first = (1 - side) * flips[0] + side * flips[1]
+    peer_last = (1 - side) * flips[1] + side * flips[0]
+
+    def want_copy(peer, slot):
+        return pltpu.make_async_remote_copy(
+            src_ref=wanted_ref,
+            dst_ref=wanted.at[me],
+            send_sem=want_send.at[slot],
+            recv_sem=want_recv.at[me],
+            device_id={"vp": peer // n_cp, "cp": lax.rem(peer, n_cp)},
+            device_id_type=pl.DeviceIdType.MESH,
+        )
+
+    def want_arrival(source):
+        return pltpu.make_async_remote_copy(
+            src_ref=wanted_ref,
+            dst_ref=wanted.at[source],
+            send_sem=want_send.at[0],
+            recv_sem=want_recv.at[source],
+            device_id={"vp": vp, "cp": cp},
+            device_id_type=pl.DeviceIdType.MESH,
+        )
+
+    def near_copy(j, target, owner_cp, a, u, peer):
+        return pltpu.make_async_remote_copy(
+            src_ref=waves[a].at[:, pl.ds(pl.multiple_of(target * part + u * piece, 128), piece)],
+            dst_ref=near.at[a, u, pl.ds(pl.multiple_of(j * chip + owner_cp * bands, bands), bands), :],
+            send_sem=near_send.at[j, target, a, u],
+            recv_sem=near_recv.at[j, owner_cp, a, u],
+            device_id={"vp": peer, "cp": target},
+            device_id_type=pl.DeviceIdType.MESH,
+        )
+
+    def near_own(a, u):
+        return pltpu.make_async_copy(
+            waves[a].at[:, pl.ds(pl.multiple_of(cp * part + u * piece, 128), piece)],
+            near.at[a, u, pl.ds(pl.multiple_of(cp * bands, bands), bands), :],
+            near_recv.at[0, cp, a, u],
+        )
+
+    def cross_copy(u):
+        return pltpu.make_async_remote_copy(
+            src_ref=sent.at[u],
+            dst_ref=came.at[u],
+            send_sem=cross_send.at[u],
+            recv_sem=cross_recv.at[u],
+            device_id={"vp": peer_last, "cp": cp},
+            device_id_type=pl.DeviceIdType.MESH,
+        )
+
+    row_bands = ROW_TILES * TV
+    slot_bands = slots * TV
+    tile_bands = row_bands + slot_bands
+
+    def give_copies(target, source_cp, u):
+        lanes = pl.ds(pl.multiple_of(source_cp * part + u * piece, 128), piece)
+        out = []
+        for j, (src, dst) in enumerate((
+            (pl.ds(0, row_bands), pl.ds(0, row_bands)),
+            (
+                pl.ds(pl.multiple_of(row_bands + target * slot_bands, 16), slot_bands),
+                pl.ds(row_bands, slot_bands),
+            ),
+        )):
+            out.append(pltpu.make_async_remote_copy(
+                src_ref=total.at[u, :, src, :],
+                dst_ref=ready.at[:, dst, lanes],
+                send_sem=give_send.at[target, u, j],
+                recv_sem=give_recv.at[source_cp, u, j],
+                device_id={"vp": vp, "cp": target},
+                device_id_type=pl.DeviceIdType.MESH,
+            ))
+        return out
+
+    for other in range(1, group):
+        want_copy(lax.rem(me + other, group), other - 1).start()
+    wanted[me] = wanted_ref[...]
+
+    def launch(u, _):
+        for a in range(2):
+            for target in range(n_cp):
+                near_copy(1, target, cp, a, u, flips[target % 2]).start()
+            for target in range(n_cp):
+                @pl.when(cp != target)
+                def _():
+                    near_copy(0, target, cp, a, u, vp).start()
+            near_own(a, u).start()
+        return 0
+
+    lax.fori_loop(0, pieces, launch, 0)
+
+    def wait_wanted(other, _):
+        want_arrival(lax.rem(me + other, group)).wait_recv()
+        return 0
+
+    lax.fori_loop(1, group, wait_wanted, 0)
+
+    band = lax.broadcasted_iota(jnp.int32, (2 * chip, wanted.shape[2]), 0)
+    band = jnp.where(band < chip, vp * chip + band, peer_first * chip + band - chip)
+
+    def chooser(device, a):
+        row = wanted[device][a : a + 1]
+        return jnp.where(band == row, 1.0, 0.0).astype(jnp.bfloat16)
+
+    def pick(u, of_chip, put):
+        for a in range(2):
+            for c in range(n_cp):
+                got_rows = lax.dot_general(
+                    chooser(of_chip * n_cp + c, a), near[a, u], (((0,), (0,)), ((), ())),
+                    preferred_element_type=jnp.float32,
+                ).astype(jnp.bfloat16)
+                if c == 0:
+                    put[u, a, pl.ds(0, row_bands), :] = got_rows[:row_bands]
+                put[u, a, pl.ds(row_bands + c * slot_bands, slot_bands), :] = got_rows[row_bands:tile_bands]
+
+    lane = 256 if piece % 256 == 0 else 128
+
+    def densities(start):
+        lanes = pl.ds(pl.multiple_of(start, lane), lane)
+        val = ready[0, :, lanes].astype(jnp.float32)
+        cond = ready[1, :, lanes].astype(jnp.float32)
         row_val = [spread(val[q * TV : (q + 1) * TV]) for q in range(ROW_TILES)]
         row_cond = [spread(cond[q * TC : (q + 1) * TC]) for q in range(ROW_TILES)]
         for q in range(ROW_TILES):
@@ -91,10 +220,80 @@
             for q in range(ROW_TILES):
                 pair_rows(rho, first + q * block, row_val[q], right_val, lanes)
                 pair_rows(rho, first + (ROW_TILES + q) * block, row_cond[q], right_cond, lanes)
+
+    def flow(t, _):
+        @pl.when(t < pieces)
+        def _():
+            for a in range(2):
+                near_own(a, t).wait()
+                for c in range(n_cp):
+                    @pl.when(cp != c)
+                    def _():
+                        near_copy(0, c, c, a, t, vp).wait_recv()
+                    near_copy(1, c, c, a, t, vp).wait_recv()
+            pick(t, peer_last, sent)
+            cross_copy(t).start()
+            pick(t, vp, picked)
+
+        u = t - 1
+
+        @pl.when(jnp.logical_and(u >= 0, u < pieces))
+        def _():
+            cross_copy(u).wait_recv()
+            for a in range(2):
+                total[u, a] = picked[u, a] + came[u, a]
+            for c in range(n_cp):
+                @pl.when(cp != c)
+                def _():
+                    for copy in give_copies(c, cp, u):
+                        copy.start()
+            lanes = pl.ds(pl.multiple_of(cp * part + u * piece, 128), piece)
+            slot_rows = pl.ds(pl.multiple_of(row_bands + cp * slot_bands, 16), slot_bands)
+            for a in range(2):
+                ready[a, pl.ds(0, row_bands), lanes] = total[u, a, pl.ds(0, row_bands), :]
+                ready[a, pl.ds(row_bands, slot_bands), lanes] = total[u, a, slot_rows, :]
+
+        w = t - 2
+
+        @pl.when(w >= 0)
+        def _():
+            for c in range(n_cp):
+                @pl.when(cp != c)
+                def _():
+                    for copy in give_copies(c, c, w):
+                        copy.wait_recv()
+
+            def each(i, _):
+                c, j = i // (piece // lane), lax.rem(i, piece // lane)
+                densities(c * part + w * piece + j * lane)
+                return 0
+
+            lax.fori_loop(0, n_cp * (piece // lane), each, 0)
+
         return 0
 
-    lax.fori_loop(0, grid // lane, densities, 0)
-    pl.semaphore_wait(barrier, n - 1)
+    lax.fori_loop(0, pieces + 2, flow, 0)
+
+    for other in range(1, group):
+        want_copy(lax.rem(me + other, group), other - 1).wait_send()
+
+    def landed(u, _):
+        for a in range(2):
+            for target in range(n_cp):
+                near_copy(1, target, cp, a, u, flips[target % 2]).wait_send()
+
+                @pl.when(cp != target)
+                def _():
+                    near_copy(0, target, cp, a, u, vp).wait_send()
+        cross_copy(u).wait_send()
+        for target in range(n_cp):
+            @pl.when(cp != target)
+            def _():
+                for copy in give_copies(target, cp, u):
+                    copy.wait_send()
+        return 0
+
+    lax.fori_loop(0, pieces, landed, 0)
 
     depth = 1024
     toward = (-1, 1)
@@ -116,8 +315,7 @@
         def _():
             first = pl.multiple_of((i // halves) * rows, rows)
             for way in range(2):
-                part = way * halves + lax.rem(i, halves)
-                column = pl.multiple_of(part * width, width)
+                column = pl.multiple_of((way * halves + lax.rem(i, halves)) * width, width)
 
                 for c in range(halves):
                     @pl.when(i == c)
@@ -146,8 +344,8 @@
                 @pl.when(far[way] > 0)
                 def _():
                     hop(way, k).wait_recv()
-                    total = own[way, k].astype(jnp.float32) + got[way, k].astype(jnp.float32)
-                    own[way, k] = total.astype(jnp.bfloat16)
+                    summed = own[way, k].astype(jnp.float32) + got[way, k].astype(jnp.float32)
+                    own[way, k] = summed.astype(jnp.bfloat16)
 
                 @pl.when(z != ends[way])
                 def _():
@@ -162,14 +360,14 @@
     def give(way, k):
         return [
             pltpu.make_async_remote_copy(
-                src_ref=sent.at[k],
+                src_ref=mine.at[k],
                 dst_ref=there.at[way],
                 send_sem=fin_send.at[k, j],
                 recv_sem=fin_recv.at[way, j],
                 device_id={"ga": k},
                 device_id_type=pl.DeviceIdType.MESH,
             )
-            for j, (sent, there) in enumerate(((ex_send, ex_got), (dr_send, dr_got)))
+            for j, (mine, there) in enumerate(((ex_send, ex_got), (dr_send, dr_got)))
         ]
 
     for way in range(2):
@@ -241,25 +439,39 @@
                         copy.wait_send()
 
 
-def make_tiles(n, slots, val, cond, basis, screen, coulomb):
+def make_tiles(sizes, slots, val, cond, wanted, basis, screen, coulomb):
+    n, n_vp, n_cp = sizes
     grid, rank = basis.shape
+    bands = val.shape[0]
     width = rank // 4
     block = TV * TC
     rows = (ROW_TILES + slots) * block
     total = (ROW_TILES + slots + 2 * ROW_TILES * slots) * block
     steps = (total // rows) * 2
     share = block // n
+    part = grid // n_cp
+    pieces = max(u for u in range(1, 5) if part % (u * 128) == 0)
+    piece = part // pieces
+    picked = (ROW_TILES + n_cp * slots) * TV
     vmem = pl.BlockSpec(memory_space=pltpu.VMEM)
+    anywhere = pl.BlockSpec(memory_space=pl.ANY)
     bf16, f32 = jnp.bfloat16, jnp.float32
     return pl.pallas_call(
-        functools.partial(tiles_kernel, n, slots),
+        functools.partial(tiles_kernel, n, n_vp, n_cp, slots),
         out_shape=(
             jax.ShapeDtypeStruct((ROW_TILES, share, slots * block), f32),
             jax.ShapeDtypeStruct((slots, share, ROW_TILES * block), f32),
         ),
-        in_specs=[vmem, vmem, pl.BlockSpec(memory_space=pl.ANY), vmem, vmem],
+        in_specs=[anywhere, anywhere, vmem, anywhere, vmem, vmem],
         out_specs=(vmem, vmem),
         scratch_shapes=[
+            pltpu.VMEM((n_vp * n_cp,) + wanted.shape, jnp.int32),
+            pltpu.VMEM((2, pieces, 2 * n_cp * bands, piece), bf16),
+            pltpu.VMEM((pieces, 2, picked, piece), bf16),
+            pltpu.VMEM((pieces, 2, picked, piece), bf16),
+            pltpu.VMEM((pieces, 2, picked, piece), bf16),
+            pltpu.VMEM((pieces, 2, picked, piece), bf16),
+            pltpu.VMEM((2, (ROW_TILES + slots) * TV, grid), bf16),
             pltpu.VMEM((grid, rank), bf16),
             pltpu.VMEM((total, grid), bf16),
             pltpu.VMEM((rows, width), f32),
@@ -271,6 +483,14 @@
             pltpu.VMEM((n, slots, share, ROW_TILES * block), bf16),
             pltpu.VMEM((2, ROW_TILES, share, slots * block), bf16),
             pltpu.VMEM((2, slots, share, ROW_TILES * block), bf16),
+            pltpu.SemaphoreType.DMA((n_vp * n_cp,)),
+            pltpu.SemaphoreType.DMA((n_vp * n_cp,)),
+            pltpu.SemaphoreType.DMA((2, n_cp, 2, pieces)),
+            pltpu.SemaphoreType.DMA((2, n_cp, 2, pieces)),
+            pltpu.SemaphoreType.DMA((pieces,)),
+            pltpu.SemaphoreType.DMA((pieces,)),
+            pltpu.SemaphoreType.DMA((n_cp, pieces, 2)),
+            pltpu.SemaphoreType.DMA((n_cp, pieces, 2)),
             pltpu.SemaphoreType.DMA((4,)),
             pltpu.SemaphoreType.DMA((2, steps)),
             pltpu.SemaphoreType.DMA((2, steps)),
@@ -280,26 +500,25 @@
         compiler_params=pltpu.CompilerParams(
             collective_id=0, has_side_effects=True, vmem_limit_bytes=67043328
         ),
-    )(val, cond, basis, screen, coulomb)
+    )(val, cond, wanted, basis, screen, coulomb)
 
 
 def shards(valence_wavefunction, cond_wave, screen_basis, screen, coulomb, window_rows, tile_owner):
     slots = tile_owner.shape[0]
     n = lax.axis_size("ga")
+    sizes = (n, lax.axis_size("vp"), lax.axis_size("cp"))
     pair_tiles = jnp.concatenate([window_rows, tile_owner])
-    val_wanted = (
-        (pair_tiles // NCT)[:, None] * TV + jnp.arange(TV, dtype=jnp.int32)[None, :]
-    ).reshape(-1)
-    cond_wanted = (
-        (pair_tiles % NCT)[:, None] * TC + jnp.arange(TC, dtype=jnp.int32)[None, :]
-    ).reshape(-1)
-    val = select_bands(
-        val_wanted, lax.all_gather(valence_wavefunction, ("vp", "cp"), axis=0, tiled=True)
-    ).astype(jnp.bfloat16)
-    cond = select_bands(
-        cond_wanted, lax.all_gather(cond_wave, ("vp", "cp"), axis=0, tiled=True)
-    ).astype(jnp.bfloat16)
-    exchange, direct = make_tiles(n, slots, val, cond, screen_basis, screen[None], coulomb[None])
+    each = jnp.arange(TV, dtype=jnp.int32)[None, :]
+    wanted = jnp.stack(
+        [
+            ((pair_tiles // NCT)[:, None] * TV + each).reshape(-1),
+            ((pair_tiles % NCT)[:, None] * TC + each).reshape(-1),
+        ]
+    )
+    wanted = jnp.pad(wanted, ((0, 6), (0, 128 - wanted.shape[1])), constant_values=-1)
+    exchange, direct = make_tiles(
+        sizes, slots, valence_wavefunction, cond_wave, wanted, screen_basis, screen[None], coulomb[None]
+    )
     v = TV // n
     exchange = exchange.reshape(2, v, TC, slots, TV, TC).transpose(0, 3, 1, 2, 4, 5)
     direct = direct.reshape(slots, v, TV, 2, TC, TC).transpose(3, 0, 1, 4, 2, 5)

time: 209 us -> 132 us (0.63)
  waiting for transfers between devices: 90 us -> 0 us
  Pallas kernels: 87.9 us -> 125 us
  between operations: 13.5 us -> 0.05 us
  matrix products: 9.92 us -> 0 us
    all_gather x2 -> x0, waiting for transfers between devices: 88.6 us -> none  [the longest x1 46.3 us: shards(): lax.all_gather(valence_wavefunction, ('vp', 'cp'), axis=0, tiled=True)]
    pallas_call x1, Pallas kernels: 87.9 us -> 125 us  [make_tiles(): pl.pallas_call(functools.partial(tiles_kernel, n, n_vp, n_cp, slots), out...]
    dot_general x2 -> x0, matrix products: 9.92 us -> none  [select_bands(): return jnp.dot(chooser, shard_part, preferred_element_type=jnp.float32)]
  transfers between devices with their start and end apart: 2 -> 0, of which waited for: 2 -> 0; matrix products, arithmetic and copies ran while one was open for 4% -> 0% of each run, Pallas kernels for 0% -> 0%
where the time goes in v2:
time: 132 us
  Pallas kernels  125 us (95%)
  other arithmetic  3.44 us (3%)
  local copies, waits for them, and re-layouts  3.09 us (2%)
    pallas_call x1, Pallas kernels, make_tiles(): pl.pallas_call(functools.partial(tiles_kernel, n, n_vp, n_cp, slots), out...  125 us

profile of v2, /device:TPU:0, one launch (start us, length us, event | category | flops | bytes accessed | tf_op | source)
XLA Modules:
  0.0 131.9 jit_solution(12900311066840489220)
XLA Ops:
  0.0 0.8 fusion.1
  0.8 0.1 iota_add_fusion
  0.8 0.1 add.71
  0.9 0.1 iota_add_fusion.1
  1.0 0.1 add.66
  1.1 0.6 pad.4.wanted_ref
  1.7 125.4 %shard_map.73 = (f32[2,16,384]{2,1,0:T(8,128)}, f32[6,16,128]{2,1,0:T(8,128)}) custom-call(bf16[64,6144]{1,0:T(8,128)(2,1)} %val_hbm.1, bf16[64,6144]{1,0:T(8,128)(2,1)} %cond_hbm.1, s32[8,128]{1,0:T(8,128)} %pad.4.wanted_ref, bf16[6144,1024]{1,0:T(8,128)(2,1)} %basis_hbm.1, f32[1,1024]{1,0:T(1,128)} %bitcast.10, f32[1,1024]{1,0:T(1,128)} %bitcast.11), custom_call_target="tpu_custom_call" | custom-call | tf_op jit(solution)/shard_map/pallas_call | solution.py:459
  127.1 0.8 broadcast_multiply_fusion
  127.9 0.4 mul.32
  128.3 1.2 reshape.198
  129.6 0.3 bitcast_subtract_fusion
  129.8 0.2 copy.9
  130.1 0.4 reshape.199
  130.5 0.7 broadcast_compare_fusion
  131.2 0.7 broadcast_select_fusion
  (2 shorter events, 0.0 us)

commit v3 on v2

--- a/solution.py
+++ b/solution.py
@@ -11,6 +11,8 @@
 NCT = 64
 LAG = 2
 ROW_TILES = 2
+PAIR = 2
+QUARTERS = 4
 
 
 def pair_rows(rho, first, left, right, lanes):
@@ -49,7 +51,8 @@
 ):
     z = lax.axis_index("ga")
     grid, rank = basis_hbm.shape
-    steps, rows, width = own.shape[1:]
+    steps, quarters, quarter, width = own.shape[1:]
+    rows = quarters * quarter
     halves = rank // (2 * width)
     ends = (0, n - 1)
     block = TV * TC
@@ -126,39 +129,48 @@
             near_recv.at[0, cp, a, u],
         )
 
-    def cross_copy(u):
-        return pltpu.make_async_remote_copy(
-            src_ref=sent.at[u],
-            dst_ref=came.at[u],
-            send_sem=cross_send.at[u],
-            recv_sem=cross_recv.at[u],
-            device_id={"vp": peer_last, "cp": cp},
-            device_id_type=pl.DeviceIdType.MESH,
-        )
-
     row_bands = ROW_TILES * TV
-    slot_bands = slots * TV
-    tile_bands = row_bands + slot_bands
-
-    def give_copies(target, source_cp, u):
+    pair_bands = PAIR * TV
+    groups = slots // PAIR
+
+    def cross_copies(u, p):
+        spans = [pl.ds(pl.multiple_of(row_bands + p * n_cp * pair_bands, 16), n_cp * pair_bands)]
+        if isinstance(p, int) and p == 0:
+            spans = [pl.ds(0, row_bands + n_cp * pair_bands)]
+        return [
+            pltpu.make_async_remote_copy(
+                src_ref=sent.at[u, :, span, :],
+                dst_ref=came.at[u, :, span, :],
+                send_sem=cross_send.at[u, p],
+                recv_sem=cross_recv.at[u, p],
+                device_id={"vp": peer_last, "cp": cp},
+                device_id_type=pl.DeviceIdType.MESH,
+            )
+            for span in spans
+        ]
+
+    def give_copies(target, source_cp, u, p):
         lanes = pl.ds(pl.multiple_of(source_cp * part + u * piece, 128), piece)
-        out = []
-        for j, (src, dst) in enumerate((
-            (pl.ds(0, row_bands), pl.ds(0, row_bands)),
+        spans = [
             (
-                pl.ds(pl.multiple_of(row_bands + target * slot_bands, 16), slot_bands),
-                pl.ds(row_bands, slot_bands),
-            ),
-        )):
-            out.append(pltpu.make_async_remote_copy(
+                pl.ds(pl.multiple_of(row_bands + (p * n_cp + target) * pair_bands, 16), pair_bands),
+                pl.ds(pl.multiple_of(row_bands + p * pair_bands, 16), pair_bands),
+                p,
+            )
+        ]
+        if isinstance(p, int) and p == 0:
+            spans.append((pl.ds(0, row_bands), pl.ds(0, row_bands), groups))
+        return [
+            pltpu.make_async_remote_copy(
                 src_ref=total.at[u, :, src, :],
                 dst_ref=ready.at[:, dst, lanes],
                 send_sem=give_send.at[target, u, j],
                 recv_sem=give_recv.at[source_cp, u, j],
                 device_id={"vp": vp, "cp": target},
                 device_id_type=pl.DeviceIdType.MESH,
-            ))
-        return out
+            )
+            for src, dst, j in spans
+        ]
 
     for other in range(1, group):
         want_copy(lax.rem(me + other, group), other - 1).start()
@@ -199,27 +211,70 @@
                 ).astype(jnp.bfloat16)
                 if c == 0:
                     put[u, a, pl.ds(0, row_bands), :] = got_rows[:row_bands]
-                put[u, a, pl.ds(row_bands + c * slot_bands, slot_bands), :] = got_rows[row_bands:tile_bands]
+                for p in range(groups):
+                    put[u, a, pl.ds(row_bands + (p * n_cp + c) * pair_bands, pair_bands), :] = got_rows[
+                        row_bands + p * pair_bands : row_bands + (p + 1) * pair_bands
+                    ]
 
     lane = 256 if piece % 256 == 0 else 128
 
-    def densities(start):
+    def densities(start, p, with_rows):
         lanes = pl.ds(pl.multiple_of(start, lane), lane)
-        val = ready[0, :, lanes].astype(jnp.float32)
-        cond = ready[1, :, lanes].astype(jnp.float32)
+        val = ready[0, pl.ds(0, row_bands), lanes].astype(jnp.float32)
+        cond = ready[1, pl.ds(0, row_bands), lanes].astype(jnp.float32)
         row_val = [spread(val[q * TV : (q + 1) * TV]) for q in range(ROW_TILES)]
         row_cond = [spread(cond[q * TC : (q + 1) * TC]) for q in range(ROW_TILES)]
-        for q in range(ROW_TILES):
-            pair_rows(rho, q * block, row_val[q], twice(cond[q * TC : (q + 1) * TC]), lanes)
-        for s in range(slots):
-            at = (ROW_TILES + s) * 8
-            slot_val, slot_cond = val[at : at + TV], cond[at : at + TC]
+        last = groups * rows
+        if with_rows:
+            for q in range(ROW_TILES):
+                pair_rows(rho, last + q * block, row_val[q], twice(cond[q * TC : (q + 1) * TC]), lanes)
+        span = pl.ds(pl.multiple_of(row_bands + p * pair_bands, 16), pair_bands)
+        val = ready[0, span, lanes].astype(jnp.float32)
+        cond = ready[1, span, lanes].astype(jnp.float32)
+        for s in range(PAIR):
+            slot_val, slot_cond = val[s * TV : (s + 1) * TV], cond[s * TC : (s + 1) * TC]
             right_val, right_cond = twice(slot_val), twice(slot_cond)
-            pair_rows(rho, (ROW_TILES + s) * block, spread(slot_val), right_cond, lanes)
-            first = (ROW_TILES + slots + 2 * ROW_TILES * s) * block
+            at = pl.multiple_of(last + (ROW_TILES + p * PAIR + s) * block, block)
+            pair_rows(rho, at, spread(slot_val), right_cond, lanes)
+            first = pl.multiple_of(p * rows + 2 * ROW_TILES * s * block, block)
             for q in range(ROW_TILES):
                 pair_rows(rho, first + q * block, row_val[q], right_val, lanes)
                 pair_rows(rho, first + (ROW_TILES + q) * block, row_cond[q], right_cond, lanes)
+
+    def hand_out(u, p):
+        lanes = pl.ds(pl.multiple_of(cp * part + u * piece, 128), piece)
+        for copy in cross_copies(u, p):
+            copy.wait_recv()
+        span = pl.ds(pl.multiple_of(row_bands + p * n_cp * pair_bands, 16), n_cp * pair_bands)
+        mine = pl.ds(pl.multiple_of(row_bands + (p * n_cp + cp) * pair_bands, 16), pair_bands)
+        home = pl.ds(pl.multiple_of(row_bands + p * pair_bands, 16), pair_bands)
+        spans = [(span, mine, home)]
+        if isinstance(p, int) and p == 0:
+            tiles = pl.ds(0, row_bands)
+            spans.append((tiles, tiles, tiles))
+        for a in range(2):
+            for span, mine, home in spans:
+                total[u, a, span, :] = picked[u, a, span, :] + came[u, a, span, :]
+                ready[a, home, lanes] = total[u, a, mine, :]
+        for c in range(n_cp):
+            @pl.when(cp != c)
+            def _():
+                for copy in give_copies(c, cp, u, p):
+                    copy.start()
+
+    def take_in(u, p):
+        for c in range(n_cp):
+            @pl.when(cp != c)
+            def _():
+                for copy in give_copies(c, c, u, p):
+                    copy.wait_recv()
+
+        def each(i, _):
+            c, j = i // (piece // lane), lax.rem(i, piece // lane)
+            densities(c * part + u * piece + j * lane, p, isinstance(p, int) and p == 0)
+            return 0
+
+        lax.fori_loop(0, n_cp * (piece // lane), each, 0)
 
     def flow(t, _):
         @pl.when(t < pieces)
@@ -232,78 +287,40 @@
                         near_copy(0, c, c, a, t, vp).wait_recv()
                     near_copy(1, c, c, a, t, vp).wait_recv()
             pick(t, peer_last, sent)
-            cross_copy(t).start()
+            for copy in cross_copies(t, 0):
+                copy.start()
             pick(t, vp, picked)
 
-        u = t - 1
-
-        @pl.when(jnp.logical_and(u >= 0, u < pieces))
-        def _():
-            cross_copy(u).wait_recv()
-            for a in range(2):
-                total[u, a] = picked[u, a] + came[u, a]
-            for c in range(n_cp):
-                @pl.when(cp != c)
-                def _():
-                    for copy in give_copies(c, cp, u):
+            @pl.when(t == pieces - 1)
+            def _():
+                def later(i, _):
+                    for copy in cross_copies(lax.rem(i, pieces), 1 + i // pieces):
                         copy.start()
-            lanes = pl.ds(pl.multiple_of(cp * part + u * piece, 128), piece)
-            slot_rows = pl.ds(pl.multiple_of(row_bands + cp * slot_bands, 16), slot_bands)
-            for a in range(2):
-                ready[a, pl.ds(0, row_bands), lanes] = total[u, a, pl.ds(0, row_bands), :]
-                ready[a, pl.ds(row_bands, slot_bands), lanes] = total[u, a, slot_rows, :]
-
-        w = t - 2
-
-        @pl.when(w >= 0)
-        def _():
-            for c in range(n_cp):
-                @pl.when(cp != c)
-                def _():
-                    for copy in give_copies(c, c, w):
-                        copy.wait_recv()
-
-            def each(i, _):
-                c, j = i // (piece // lane), lax.rem(i, piece // lane)
-                densities(c * part + w * piece + j * lane)
-                return 0
-
-            lax.fori_loop(0, n_cp * (piece // lane), each, 0)
+                    return 0
+
+                lax.fori_loop(0, pieces * (groups - 1), later, 0)
+
+        @pl.when(jnp.logical_and(t >= 1, t <= pieces))
+        def _():
+            hand_out(t - 1, 0)
+
+        @pl.when(t >= 2)
+        def _():
+            take_in(t - 2, 0)
 
         return 0
 
     lax.fori_loop(0, pieces + 2, flow, 0)
-
-    for other in range(1, group):
-        want_copy(lax.rem(me + other, group), other - 1).wait_send()
-
-    def landed(u, _):
-        for a in range(2):
-            for target in range(n_cp):
-                near_copy(1, target, cp, a, u, flips[target % 2]).wait_send()
-
-                @pl.when(cp != target)
-                def _():
-                    near_copy(0, target, cp, a, u, vp).wait_send()
-        cross_copy(u).wait_send()
-        for target in range(n_cp):
-            @pl.when(cp != target)
-            def _():
-                for copy in give_copies(target, cp, u):
-                    copy.wait_send()
-        return 0
-
-    lax.fori_loop(0, pieces, landed, 0)
 
     depth = 1024
     toward = (-1, 1)
 
-    def hop(way, k):
+    def hop(way, k, h):
         return pltpu.make_async_remote_copy(
-            src_ref=own.at[way, k],
-            dst_ref=got.at[way, k],
-            send_sem=send_sem.at[way, k],
-            recv_sem=recv_sem.at[way, k],
+            src_ref=own.at[way, k, h],
+            dst_ref=got.at[way, k, h],
+            send_sem=send_sem.at[way, k, h],
+            recv_sem=recv_sem.at[way, k, h],
             device_id={"ga": lax.rem(z + toward[way] + n, n)},
             device_id_type=pl.DeviceIdType.MESH,
         )
@@ -334,22 +351,42 @@
                     return 0
 
                 lax.fori_loop(0, grid // depth, deep, 0)
-                own[way, i] = acc[...].astype(jnp.bfloat16)
-
-        for way in range(2):
-            k = i - LAG * far[way]
-
-            @pl.when(jnp.logical_and(k >= 0, k < steps))
-            def _():
-                @pl.when(far[way] > 0)
+                for h in range(QUARTERS):
+                    own[way, i, h] = acc[pl.ds(h * (rows // QUARTERS), rows // QUARTERS), :].astype(jnp.bfloat16)
+
+        for h in range(QUARTERS):
+            for way in range(2):
+                k = i - LAG * far[way]
+
+                @pl.when(jnp.logical_and(k >= 0, k < steps))
                 def _():
-                    hop(way, k).wait_recv()
-                    summed = own[way, k].astype(jnp.float32) + got[way, k].astype(jnp.float32)
-                    own[way, k] = summed.astype(jnp.bfloat16)
-
-                @pl.when(z != ends[way])
-                def _():
-                    hop(way, k).start()
+                    @pl.when(far[way] > 0)
+                    def _():
+                        hop(way, k, h).wait_recv()
+                        summed = own[way, k, h].astype(jnp.float32) + got[way, k, h].astype(jnp.float32)
+                        own[way, k, h] = summed.astype(jnp.bfloat16)
+
+                    @pl.when(z != ends[way])
+                    def _():
+                        hop(way, k, h).start()
+
+        after = 1 + i // halves
+
+        @pl.when(jnp.logical_and(after < groups, lax.rem(i, halves) == 0))
+        def _():
+            def out(u, _):
+                hand_out(u, after)
+                return 0
+
+            lax.fori_loop(0, pieces, out, 0)
+
+        @pl.when(jnp.logical_and(after < groups, lax.rem(i, halves) == halves - 1))
+        def _():
+            def into(u, _):
+                take_in(u, after)
+                return 0
+
+            lax.fori_loop(0, pieces, into, 0)
 
         return 0
 
@@ -376,19 +413,18 @@
             exchange = jnp.zeros(ex_own.shape, jnp.float32)
             for c in range(halves):
                 weight = coulomb_ref[:, pl.ds((way * halves + c) * width, width)]
-                left = own[way, c, pl.ds(0, ROW_TILES * block), :]
-                right = own[way, c, pl.ds(ROW_TILES * block, slots * block), :]
+                whole = own[way, groups * halves + c].reshape(rows, width)
+                left, right = whole[: ROW_TILES * block], whole[ROW_TILES * block :]
                 exchange += weighted_dot(left, weight, right)
             ex_own[...] = exchange
             wide = ROW_TILES * block
             for s in range(slots):
-                first = (ROW_TILES + slots + 2 * ROW_TILES * s) * block
-                job, at = first // rows, first % rows
+                job, at = s // PAIR, (s % PAIR) * 2 * wide
                 direct = jnp.zeros((wide, wide), jnp.float32)
                 for c in range(halves):
                     weight = screen_ref[:, pl.ds((way * halves + c) * width, width)]
-                    left = own[way, job * halves + c, pl.ds(at, wide), :]
-                    right = own[way, job * halves + c, pl.ds(at + wide, wide), :]
+                    whole = own[way, job * halves + c].reshape(rows, width)
+                    left, right = whole[at : at + wide], whole[at + wide : at + 2 * wide]
                     direct += weighted_dot(left, weight, right)
                 column = lax.broadcasted_iota(jnp.int32, (block, wide), 1)
                 dr_own[s] = jnp.where(column < block, direct[:block], direct[block:])
@@ -426,7 +462,8 @@
         @pl.when(z != ends[way])
         def _():
             def drain(k, _):
-                hop(way, k).wait_send()
+                for h in range(QUARTERS):
+                    hop(way, k, h).wait_send()
                 return 0
 
             lax.fori_loop(0, steps, drain, 0)
@@ -437,6 +474,29 @@
                 if k != ends[way]:
                     for copy in give(way, k):
                         copy.wait_send()
+
+    for other in range(1, group):
+        want_copy(lax.rem(me + other, group), other - 1).wait_send()
+
+    def landed(u, _):
+        for a in range(2):
+            for target in range(n_cp):
+                near_copy(1, target, cp, a, u, flips[target % 2]).wait_send()
+
+                @pl.when(cp != target)
+                def _():
+                    near_copy(0, target, cp, a, u, vp).wait_send()
+        for p in range(groups):
+            for copy in cross_copies(u, p):
+                copy.wait_send()
+            for target in range(n_cp):
+                @pl.when(cp != target)
+                def _():
+                    for copy in give_copies(target, cp, u, p):
+                        copy.wait_send()
+        return 0
+
+    lax.fori_loop(0, pieces, landed, 0)
 
 
 def make_tiles(sizes, slots, val, cond, wanted, basis, screen, coulomb):
@@ -475,8 +535,8 @@
             pltpu.VMEM((grid, rank), bf16),
             pltpu.VMEM((total, grid), bf16),
             pltpu.VMEM((rows, width), f32),
-            pltpu.VMEM((2, steps, rows, width), bf16),
-            pltpu.VMEM((2, steps, rows, width), bf16),
+            pltpu.VMEM((2, steps, QUARTERS, rows // QUARTERS, width), bf16),
+            pltpu.VMEM((2, steps, QUARTERS, rows // QUARTERS, width), bf16),
             pltpu.VMEM((ROW_TILES * block, slots * block), f32),
             pltpu.VMEM((slots, block, ROW_TILES * block), f32),
             pltpu.VMEM((n, ROW_TILES, share, slots * block), bf16),
@@ -487,13 +547,13 @@
             pltpu.SemaphoreType.DMA((n_vp * n_cp,)),
             pltpu.SemaphoreType.DMA((2, n_cp, 2, pieces)),
             pltpu.SemaphoreType.DMA((2, n_cp, 2, pieces)),
-            pltpu.SemaphoreType.DMA((pieces,)),
-            pltpu.SemaphoreType.DMA((pieces,)),
-            pltpu.SemaphoreType.DMA((n_cp, pieces, 2)),
-            pltpu.SemaphoreType.DMA((n_cp, pieces, 2)),
+            pltpu.SemaphoreType.DMA((pieces, slots // PAIR)),
+            pltpu.SemaphoreType.DMA((pieces, slots // PAIR)),
+            pltpu.SemaphoreType.DMA((n_cp, pieces, slots // PAIR + 1)),
+            pltpu.SemaphoreType.DMA((n_cp, pieces, slots // PAIR + 1)),
             pltpu.SemaphoreType.DMA((4,)),
-            pltpu.SemaphoreType.DMA((2, steps)),
-            pltpu.SemaphoreType.DMA((2, steps)),
+            pltpu.SemaphoreType.DMA((2, steps, QUARTERS)),
+            pltpu.SemaphoreType.DMA((2, steps, QUARTERS)),
             pltpu.SemaphoreType.DMA((n, 2)),
             pltpu.SemaphoreType.DMA((2, 2)),
         ],

time: 132 us -> 131 us (level)
  no operation moved by 1% of the time
where the time goes in v3:
time: 131 us
  Pallas kernels  124 us (95%)
  other arithmetic  3.44 us (3%)
  local copies, waits for them, and re-layouts  3.09 us (2%)
    pallas_call x1, Pallas kernels, make_tiles(): pl.pallas_call(functools.partial(tiles_kernel, n, n_vp, n_cp, slots), out...  124 us

profile of v3, /device:TPU:0, one launch (start us, length us, event | category | flops | bytes accessed | tf_op | source)
XLA Modules:
  0.0 130.8 jit_solution(8109970110408893550)
XLA Ops:
  0.0 0.8 fusion.1
  0.8 0.1 iota_add_fusion
  0.8 0.1 add.71
  0.9 0.1 iota_add_fusion.1
  1.0 0.1 add.66
  1.1 0.6 pad.4.wanted_ref
  1.7 124.2 %shard_map.73 = (f32[2,16,384]{2,1,0:T(8,128)}, f32[6,16,128]{2,1,0:T(8,128)}) custom-call(bf16[64,6144]{1,0:T(8,128)(2,1)} %val_hbm.1, bf16[64,6144]{1,0:T(8,128)(2,1)} %cond_hbm.1, s32[8,128]{1,0:T(8,128)} %pad.4.wanted_ref, bf16[6144,1024]{1,0:T(8,128)(2,1)} %basis_hbm.1, f32[1,1024]{1,0:T(1,128)} %bitcast.10, f32[1,1024]{1,0:T(1,128)} %bitcast.11), custom_call_target="tpu_custom_call" | custom-call | tf_op jit(solution)/shard_map/pallas_call | solution.py:519
  125.9 0.8 broadcast_multiply_fusion
  126.7 0.4 mul.32
  127.1 1.2 reshape.198
  128.4 0.3 bitcast_subtract_fusion
  128.7 0.2 copy.9
  128.9 0.4 reshape.199
  129.3 0.7 broadcast_compare_fusion
  130.1 0.7 broadcast_select_fusion
  (2 shorter events, 0.0 us)

commit v4 on v3

--- a/solution.py
+++ b/solution.py
@@ -9,7 +9,7 @@
 TV = 8
 TC = 8
 NCT = 64
-LAG = 2
+LAG = 1
 ROW_TILES = 2
 PAIR = 2
 QUARTERS = 4
@@ -45,7 +45,7 @@
 
 def tiles_kernel(
     n, n_vp, n_cp, slots, val_hbm, cond_hbm, wanted_ref, basis_hbm, screen_ref, coulomb_ref,
-    exch_ref, direct_ref, wanted, near, picked, sent, came, total, ready, basis, rho, acc, own, got, ex_own, dr_own, ex_send, dr_send, ex_got, dr_got,
+    exch_ref, direct_ref, wanted, chosen, near, picked, sent, came, total, ready, basis, rho, acc, own, got, ex_own, dr_own, ex_send, dr_send, ex_got, dr_got,
     want_send, want_recv, near_send, near_recv, cross_send, cross_recv, give_send, give_recv,
     basis_sem, send_sem, recv_sem, fin_send, fin_recv,
 ):
@@ -198,23 +198,29 @@
     band = lax.broadcasted_iota(jnp.int32, (2 * chip, wanted.shape[2]), 0)
     band = jnp.where(band < chip, vp * chip + band, peer_first * chip + band - chip)
 
-    def chooser(device, a):
-        row = wanted[device][a : a + 1]
-        return jnp.where(band == row, 1.0, 0.0).astype(jnp.bfloat16)
-
-    def pick(u, of_chip, put):
+    slot_rows = wanted.shape[2] // 2
+    first_half = lax.broadcasted_iota(jnp.int32, (1, wanted.shape[2]), 1) < slot_rows
+    for a in range(2):
+        for j, of_chip in enumerate((peer_last, vp)):
+            for c in range(0, n_cp, 2):
+                device = of_chip * n_cp + c
+                row = jnp.where(first_half, wanted[device][a : a + 1], wanted[device + 1][a : a + 1])
+                hot = jnp.where(band == row, 1.0, 0.0).T
+                at = (j * n_cp + c) * slot_rows
+                chosen[a, pl.ds(at, 2 * slot_rows), :] = hot.astype(jnp.bfloat16)
+
+    def pick(u):
         for a in range(2):
-            for c in range(n_cp):
-                got_rows = lax.dot_general(
-                    chooser(of_chip * n_cp + c, a), near[a, u], (((0,), (0,)), ((), ())),
-                    preferred_element_type=jnp.float32,
-                ).astype(jnp.bfloat16)
-                if c == 0:
-                    put[u, a, pl.ds(0, row_bands), :] = got_rows[:row_bands]
-                for p in range(groups):
-                    put[u, a, pl.ds(row_bands + (p * n_cp + c) * pair_bands, pair_bands), :] = got_rows[
-                        row_bands + p * pair_bands : row_bands + (p + 1) * pair_bands
-                    ]
+            found = jnp.dot(chosen[a], near[a, u], preferred_element_type=jnp.float32).astype(jnp.bfloat16)
+            for j, put in enumerate((sent, picked)):
+                for c in range(n_cp):
+                    got_rows = found[(j * n_cp + c) * slot_rows : (j * n_cp + c + 1) * slot_rows]
+                    if c == 0:
+                        put[u, a, pl.ds(0, row_bands), :] = got_rows[:row_bands]
+                    for p in range(groups):
+                        put[u, a, pl.ds(row_bands + (p * n_cp + c) * pair_bands, pair_bands), :] = got_rows[
+                            row_bands + p * pair_bands : row_bands + (p + 1) * pair_bands
+                        ]
 
     lane = 256 if piece % 256 == 0 else 128
 
@@ -286,10 +292,9 @@
                     def _():
                         near_copy(0, c, c, a, t, vp).wait_recv()
                     near_copy(1, c, c, a, t, vp).wait_recv()
-            pick(t, peer_last, sent)
+            pick(t)
             for copy in cross_copies(t, 0):
                 copy.start()
-            pick(t, vp, picked)
 
             @pl.when(t == pieces - 1)
             def _():
@@ -369,6 +374,24 @@
                     @pl.when(z != ends[way])
                     def _():
                         hop(way, k, h).start()
+
+        for way in range(2):
+            k = i - LAG * far[way]
+            p = k // halves
+            done = jnp.logical_and(k >= 0, jnp.logical_and(lax.rem(k, halves) == halves - 1, p < groups))
+
+            @pl.when(jnp.logical_and(z == ends[way], done))
+            def _():
+                wide = ROW_TILES * block
+                for s in range(PAIR):
+                    direct = jnp.zeros((wide, wide), jnp.float32)
+                    for c in range(halves):
+                        weight = screen_ref[:, pl.ds((way * halves + c) * width, width)]
+                        whole = own[way, p * halves + c].reshape(rows, width)
+                        at = s * 2 * wide
+                        direct += weighted_dot(whole[at : at + wide], weight, whole[at + wide : at + 2 * wide])
+                    column = lax.broadcasted_iota(jnp.int32, (block, wide), 1)
+                    dr_own[p * PAIR + s] = jnp.where(column < block, direct[:block], direct[block:])
 
         after = 1 + i // halves
 
@@ -417,17 +440,6 @@
                 left, right = whole[: ROW_TILES * block], whole[ROW_TILES * block :]
                 exchange += weighted_dot(left, weight, right)
             ex_own[...] = exchange
-            wide = ROW_TILES * block
-            for s in range(slots):
-                job, at = s // PAIR, (s % PAIR) * 2 * wide
-                direct = jnp.zeros((wide, wide), jnp.float32)
-                for c in range(halves):
-                    weight = screen_ref[:, pl.ds((way * halves + c) * width, width)]
-                    whole = own[way, job * halves + c].reshape(rows, width)
-                    left, right = whole[at : at + wide], whole[at + wide : at + 2 * wide]
-                    direct += weighted_dot(left, weight, right)
-                column = lax.broadcasted_iota(jnp.int32, (block, wide), 1)
-                dr_own[s] = jnp.where(column < block, direct[:block], direct[block:])
             for k in range(n):
                 if k != ends[way]:
                     for q in range(ROW_TILES):
@@ -526,6 +538,7 @@
         out_specs=(vmem, vmem),
         scratch_shapes=[
             pltpu.VMEM((n_vp * n_cp,) + wanted.shape, jnp.int32),
+            pltpu.VMEM((2, n_cp * wanted.shape[1], 2 * n_cp * bands), bf16),
             pltpu.VMEM((2, pieces, 2 * n_cp * bands, piece), bf16),
             pltpu.VMEM((pieces, 2, picked, piece), bf16),
             pltpu.VMEM((pieces, 2, picked, piece), bf16),
@@ -575,7 +588,7 @@
             ((pair_tiles % NCT)[:, None] * TC + each).reshape(-1),
         ]
     )
-    wanted = jnp.pad(wanted, ((0, 6), (0, 128 - wanted.shape[1])), constant_values=-1)
+    wanted = jnp.pad(jnp.concatenate([wanted, wanted], axis=1), ((0, 6), (0, 0)), constant_values=-1)
     exchange, direct = make_tiles(
         sizes, slots, valence_wavefunction, cond_wave, wanted, screen_basis, screen[None], coulomb[None]
     )

time: 131 us -> 124 us (0.947)
  Pallas kernels: 124 us -> 117 us
    pallas_call x1, Pallas kernels: 124 us -> 117 us  [make_tiles(): pl.pallas_call(functools.partial(tiles_kernel, n, n_vp, n_cp, slots), out...]
where the time goes in v4:
time: 124 us; the launch traced here: 123 us
  Pallas kernels  117 us (94%)
  other arithmetic  3.5 us (3%)
  local copies, waits for them, and re-layouts  3.09 us (2%)
    pallas_call x1, Pallas kernels, make_tiles(): pl.pallas_call(functools.partial(tiles_kernel, n, n_vp, n_cp, slots), out...  117 us

profile of v4, /device:TPU:0, one launch (start us, length us, event | category | flops | bytes accessed | tf_op | source)
XLA Modules:
  0.0 123.3 jit_solution(2907228189691352504)
XLA Ops:
  0.0 0.8 fusion.1
  0.8 0.1 iota_add_fusion
  0.8 0.1 add.71
  0.9 0.1 iota_add_fusion.1
  1.0 0.1 add.66
  1.1 0.1 add_add_fusion
  1.1 0.6 pad.4.wanted_ref
  1.8 116.7 %shard_map.73 = (f32[2,16,384]{2,1,0:T(8,128)}, f32[6,16,128]{2,1,0:T(8,128)}) custom-call(bf16[64,6144]{1,0:T(8,128)(2,1)} %val_hbm.1, bf16[64,6144]{1,0:T(8,128)(2,1)} %cond_hbm.1, s32[8,128]{1,0:T(8,128)} %pad.4.wanted_ref, bf16[6144,1024]{1,0:T(8,128)(2,1)} %basis_hbm.1, f32[1,1024]{1,0:T(1,128)} %bitcast.10, f32[1,1024]{1,0:T(1,128)} %bitcast.11), custom_call_target="tpu_custom_call" | custom-call | tf_op jit(solution)/shard_map/pallas_call | solution.py:531
  118.5 0.8 broadcast_multiply_fusion
  119.3 0.4 mul.32
  119.7 1.2 %reshape.198 = f32[6,2,8,2,8,8]{5,4,3,2,1,0:T(8,128)S(1)} reshape(f32[6,16,128]{2,1,0:T(8,128)} %get-tuple-element.8) | data formatting | bytes 98304 | tf_op jit(solution)/shard_map/reshape | solution.py:597
  121.0 0.3 bitcast_subtract_fusion
  121.2 0.2 copy.9
  121.5 0.4 reshape.199
  121.9 0.7 broadcast_compare_fusion
  122.6 0.7 broadcast_select_fusion
  (1 shorter events, 0.0 us)

commit v5 on v4

--- a/solution.py
+++ b/solution.py
@@ -12,7 +12,7 @@
 LAG = 1
 ROW_TILES = 2
 PAIR = 2
-QUARTERS = 4
+QUARTERS = 8
 
 
 def pair_rows(rho, first, left, right, lanes):
@@ -332,6 +332,21 @@
 
     far = (n - 1 - z, z)
 
+    def relay(i, way, h):
+        k = i - LAG * far[way]
+
+        @pl.when(jnp.logical_and(k >= 0, k < steps))
+        def _():
+            @pl.when(far[way] > 0)
+            def _():
+                hop(way, k, h).wait_recv()
+                summed = own[way, k, h].astype(jnp.float32) + got[way, k, h].astype(jnp.float32)
+                own[way, k, h] = summed.astype(jnp.bfloat16)
+
+            @pl.when(z != ends[way])
+            def _():
+                hop(way, k, h).start()
+
     def step(i, _):
         @pl.when(i < steps)
         def _():
@@ -358,22 +373,20 @@
                 lax.fori_loop(0, grid // depth, deep, 0)
                 for h in range(QUARTERS):
                     own[way, i, h] = acc[pl.ds(h * (rows // QUARTERS), rows // QUARTERS), :].astype(jnp.bfloat16)
-
-        for h in range(QUARTERS):
-            for way in range(2):
-                k = i - LAG * far[way]
-
-                @pl.when(jnp.logical_and(k >= 0, k < steps))
-                def _():
-                    @pl.when(far[way] > 0)
-                    def _():
-                        hop(way, k, h).wait_recv()
-                        summed = own[way, k, h].astype(jnp.float32) + got[way, k, h].astype(jnp.float32)
-                        own[way, k, h] = summed.astype(jnp.bfloat16)
-
-                    @pl.when(z != ends[way])
-                    def _():
-                        hop(way, k, h).start()
+                if way == 0:
+                    for h in range(QUARTERS):
+                        relay(i, 0, h)
+
+        @pl.when(i < steps)
+        def _():
+            for h in range(QUARTERS):
+                relay(i, 1, h)
+
+        @pl.when(i >= steps)
+        def _():
+            for h in range(QUARTERS):
+                for way in range(2):
+                    relay(i, way, h)
 
         for way in range(2):
             k = i - LAG * far[way]

time: 124 us -> 125 us (level)
    pallas_call x1, Pallas kernels: 117 us -> 118 us  [make_tiles(): pl.pallas_call(functools.partial(tiles_kernel, n, n_vp, n_cp, slots), out...]
where the time goes in v5:
time: 125 us
  Pallas kernels  118 us (94%)
  other arithmetic  3.5 us (3%)
  local copies, waits for them, and re-layouts  3.09 us (2%)
    pallas_call x1, Pallas kernels, make_tiles(): pl.pallas_call(functools.partial(tiles_kernel, n, n_vp, n_cp, slots), out...  118 us

profile of v5, /device:TPU:0, one launch (start us, length us, event | category | flops | bytes accessed | tf_op | source)
XLA Modules:
  0.0 124.8 jit_solution(14423733102161314187)
XLA Ops:
  0.0 0.8 fusion.1
  0.8 0.1 iota_add_fusion
  0.8 0.1 add.71
  0.9 0.1 iota_add_fusion.1
  1.0 0.1 add.66
  1.1 0.1 add_add_fusion
  1.1 0.6 pad.4.wanted_ref
  1.8 118.1 %shard_map.73 = (f32[2,16,384]{2,1,0:T(8,128)}, f32[6,16,128]{2,1,0:T(8,128)}) custom-call(bf16[64,6144]{1,0:T(8,128)(2,1)} %val_hbm.1, bf16[64,6144]{1,0:T(8,128)(2,1)} %cond_hbm.1, s32[8,128]{1,0:T(8,128)} %pad.4.wanted_ref, bf16[6144,1024]{1,0:T(8,128)(2,1)} %basis_hbm.1, f32[1,1024]{1,0:T(1,128)} %bitcast.10, f32[1,1024]{1,0:T(1,128)} %bitcast.11), custom_call_target="tpu_custom_call" | custom-call | tf_op jit(solution)/shard_map/pallas_call | solution.py:544
  119.9 0.8 broadcast_multiply_fusion
  120.7 0.4 mul.32
  121.1 1.2 reshape.198
  122.4 0.3 bitcast_subtract_fusion
  122.7 0.2 copy.9
  122.9 0.4 reshape.199
  123.3 0.7 broadcast_compare_fusion
  124.1 0.7 broadcast_select_fusion
  (1 shorter events, 0.0 us)
